TPU v7x, 512 devices: a whole 4x4x16 slice. The times are simulated.
512 devices in a mesh: ka: 128 (over z_lo, y, x, core), pb: 4 (over z_hi).
Axes of the slice: x: 4, y: 4, z: 16 (z_hi: 4, z_lo: 4; z = z_hi * 4 + z_lo), core: 2. Of those that a mesh axis runs over, the one named last changes fastest.
Arguments:
- coupling: float32 [256, 16, 2, 64, 128], P('ka', 'pb'), may hold values from -6 to 6
- gauge: float32 [256, 64, 128], P('ka'), may hold values from -0.5 to 0.5
- kq_index: int32 [16, 256], P(None, 'ka'), may hold values from 0 to 255, as said below
- fine_coords: int32 [3, 256], replicated, may hold values from 0 to 31
- eig_right: float32 [256, 64, 128], P('ka'), may hold values from -0.5 to 0.5
- eig_left: float32 [256, 16, 64, 128], P('ka', 'pb'), may hold values from -0.5 to 0.5
- energy_k: float32 [256, 64], P('ka'), may hold values from -4 to 4
- energy_kq: float32 [256, 16, 64], P('ka', 'pb'), may hold values from -4 to 4
- occupied: int32 [256, 16, 64], P('ka', 'pb'), may hold values 0 or 1
- frequency: float32 [16, 2], P('pb'), may hold values from 0.02 to 0.12
Outputs:
- self_energy: float32 [256, 64], P('ka')
Inputs may be any that keep to these rules, and one draw needn't show every extreme that they name: kq_index[q, k] is the number of the coarse point k displaced by the q-th window point's offset on the periodic 8 x 8 x 4 grid; for each q it is a permutation of the coarse points. Among the offsets are (4, 0, 0) and (0, 0, 3).
All inputs are finite; a program needn't handle non-finite values. No bound on the sum of `occupied` on one device may be relied on, other than what follows from the above.
Results may differ from a plain program's by a relative error of at most 0.0001.
Values sent between devices are 32-bit elements; how exact they have to be, the bound alone decides.
No kernel may reach another device: no remote copies, remote signals or barrier semaphores. Data moves between devices by JAX's collectives and lax.ppermute only.
A program may use at most 64 MiB of HBM per device.

v0:
```python
import math
import jax
import jax.numpy as jnp
from jax import lax
from jax.sharding import Mesh
from jax.sharding import PartitionSpec as P

GX = 8
GY = 8
GZ = 4
FG = 32
NK = 256
KA = ("ka_0", "ka_1", "ka_2", "ka_3")
PRECISE = lax.Precision.HIGHEST
BROADEN = 0.1
THERMAL = 0.05


def sent_to_all(x, axis):
    devices = lax.axis_size(axis)
    return lax.all_to_all(jnp.broadcast_to(x[None], (devices, *x.shape)), axis, 0, 0, tiled=True)


def joined_along(parts, dim):
    parts = jnp.moveaxis(parts, 0, dim)
    lengths = parts.shape
    return parts.reshape(*lengths[:dim], lengths[dim] * lengths[dim + 1], *lengths[dim + 2 :])


def gather_axes(x, axes, dim):
    far, near = axes
    first = sent_to_all(x, far)
    parts = jnp.swapaxes(sent_to_all(first, near), 0, 1)
    return joined_along(parts.reshape(-1, *x.shape), dim)


def taken_together(x, axis):
    return sent_to_all(x, axis).sum(axis=0)


def product(left_matrix, right_matrix):
    return jnp.dot(left_matrix, right_matrix, precision=PRECISE, preferred_element_type=jnp.float32)


def mult(pattern, first, second):
    return jnp.einsum(pattern, first, second, precision=PRECISE)


def phase_tables(fine_coords):
    points = jnp.arange(NK, dtype=jnp.int32)
    along_first = points // (GY * GZ)
    along_second = points // GZ % GY
    along_third = points % GZ
    cell_first = along_first - GX // 2
    cell_second = along_second - GY // 2
    cell_third = along_third - GZ // 2
    coarse_index = (
        cell_first[:, None] * along_first[None, :] * (GY * GZ)
        + cell_second[:, None] * along_second[None, :] * (GX * GZ)
        + cell_third[:, None] * along_third[None, :] * (GX * GY)
    ) % NK
    coarse_angles = coarse_index.astype(jnp.float32) * (2.0 * math.pi / NK)
    fine_index = (
        fine_coords[0][:, None] * cell_first[None, :]
        + fine_coords[1][:, None] * cell_second[None, :]
        + fine_coords[2][:, None] * cell_third[None, :]
    ) % FG
    fine_angles = fine_index.astype(jnp.float32) * (2.0 * math.pi / FG)
    return (
        jnp.cos(coarse_angles) / NK,
        -jnp.sin(coarse_angles) / NK,
        jnp.cos(fine_angles),
        jnp.sin(fine_angles),
    )


def right_block(matrix):
    orbitals = matrix.shape[-2]
    real_part = matrix[..., :orbitals]
    imag_part = matrix[..., orbitals:]
    upper_half = jnp.concatenate([real_part, imag_part], -1)
    lower_half = jnp.concatenate([-imag_part, real_part], -1)
    return jnp.concatenate([upper_half, lower_half], -2)


def sectioned(cols_real, cols_imag, tables):
    coarse_real, coarse_imag, fine_cos, fine_sin = tables
    space_real = product(coarse_real, cols_real) - product(coarse_imag, cols_imag)
    space_imag = product(coarse_real, cols_imag) + product(coarse_imag, cols_real)
    fine_real_part = product(fine_cos, space_real) - product(fine_sin, space_imag)
    fine_imag_part = product(fine_cos, space_imag) + product(fine_sin, space_real)
    return (fine_real_part, fine_imag_part)


def self_terms(strength, energy_k, energy_kq, occupied, frequency):
    phonon = frequency[None, :, :, None, None]
    bose_factor = 1.0 / (jnp.exp(phonon / THERMAL) - 1.0)
    filled = occupied.astype(jnp.float32)[:, :, None, :, None]
    energy_gap = energy_k[:, None, None, None, :] - energy_kq[:, :, None, :, None]
    shifted_up = energy_gap + phonon
    shifted_down = energy_gap - phonon
    kernel = (bose_factor + filled) * shifted_up / (shifted_up * shifted_up + BROADEN * BROADEN)
    kernel = kernel + (bose_factor + 1.0 - filled) * shifted_down / (
        shifted_down * shifted_down + BROADEN * BROADEN
    )
    return jnp.sum(strength / (2.0 * phonon) * kernel, axis=(1, 2, 3))


def select_rows(wanted, block_rows):
    positions = jnp.arange(block_rows.shape[0], dtype=jnp.int32)
    onehot = (wanted[:, None] == positions[None, :]).astype(jnp.float32)
    return product(onehot, block_rows.reshape(block_rows.shape[0], -1))


def shards(
    coupling,
    gauge,
    kq_index,
    fine_coords,
    eig_right,
    eig_left,
    energy_k,
    energy_kq,
    occupied,
    frequency,
):
    coarse_rows = coupling.shape[0]
    qpoint_rows = coupling.shape[1]
    branches = coupling.shape[2]
    orbitals = coupling.shape[3]
    pb_count = lax.axis_size("pb")
    tables = phase_tables(fine_coords)
    fine_total = fine_coords.shape[1]
    quarter = orbitals // pb_count
    own_part = lax.dynamic_slice_in_dim(gauge, lax.axis_index("pb") * quarter, quarter, 1)
    wanted = kq_index.T.reshape(-1)
    picked = select_rows(wanted, gather_axes(own_part, (("ka_0", "ka_1", "ka_2"), "ka_3"), 0))
    shares = picked.reshape(coarse_rows, kq_index.shape[0], quarter, 2 * orbitals)
    left_gauge = lax.all_to_all(shares, "pb", split_axis=1, concat_axis=2, tiled=True)
    right_gauge = mult("kqbjc,kcd->kqbjd", coupling, right_block(gauge))
    right_real = right_gauge[..., :orbitals]
    right_imag = right_gauge[..., orbitals:]
    left_real = left_gauge[..., :orbitals]
    left_imag = left_gauge[..., orbitals:]
    wannier_real = mult("kqjm,kqbjn->kqbmn", left_real, right_real) + mult(
        "kqjm,kqbjn->kqbmn", left_imag, right_imag
    )
    wannier_imag = mult("kqjm,kqbjn->kqbmn", left_real, right_imag) - mult(
        "kqjm,kqbjn->kqbmn", left_imag, right_real
    )
    pair_major = jnp.stack([wannier_real, wannier_imag], 1).reshape(
        coarse_rows, 2, qpoint_rows, branches, orbitals * orbitals
    )
    arrived_block = lax.all_to_all(pair_major, KA, split_axis=4, concat_axis=0, tiled=True)
    columns = arrived_block.reshape(arrived_block.shape[0], 2, -1)
    fine_real_part, fine_imag_part = sectioned(columns[:, 0], columns[:, 1], tables)
    fine_cols = jnp.stack([fine_real_part, fine_imag_part], 1).reshape(
        (fine_total, 2) + arrived_block.shape[2:]
    )
    fine_coupling = lax.all_to_all(fine_cols, KA, split_axis=0, concat_axis=4, tiled=True)
    fine_rows = fine_coupling.shape[0]
    arrived_parts = fine_coupling.reshape(fine_rows, 2, qpoint_rows, branches, orbitals, orbitals)
    coupled_real = arrived_parts[:, 0]
    coupled_imag = arrived_parts[:, 1]
    vector_real = eig_right[..., :orbitals]
    vector_imag = eig_right[..., orbitals:]
    half_real = mult("fqbjc,fcd->fqbjd", coupled_real, vector_real) - mult(
        "fqbjc,fcd->fqbjd", coupled_imag, vector_imag
    )
    half_imag = mult("fqbjc,fcd->fqbjd", coupled_real, vector_imag) + mult(
        "fqbjc,fcd->fqbjd", coupled_imag, vector_real
    )
    outer_real = eig_left[..., :orbitals]
    outer_imag = eig_left[..., orbitals:]
    bloch_real = mult("fqjm,fqbjn->fqbmn", outer_real, half_real) + mult(
        "fqjm,fqbjn->fqbmn", outer_imag, half_imag
    )
    bloch_imag = mult("fqjm,fqbjn->fqbmn", outer_real, half_imag) - mult(
        "fqjm,fqbjn->fqbmn", outer_imag, half_real
    )
    strength = bloch_real * bloch_real + bloch_imag * bloch_imag
    contrib = self_terms(strength, energy_k, energy_kq, occupied, frequency)
    summed = taken_together(contrib, "pb")
    return summed / (qpoint_rows * pb_count * orbitals)


def solution(mesh):
    split = Mesh(
        mesh.devices.reshape(4, 4, 4, 2, mesh.shape["pb"]), ("ka_0", "ka_1", "ka_2", "ka_3", "pb")
    )
    return jax.shard_map(
        shards,
        mesh=split,
        in_specs=(
            P(KA, "pb", None, None, None),
            P(KA, None, None),
            P(None, KA),
            P(),
            P(KA, None, None),
            P(KA, "pb", None, None),
            P(KA, None),
            P(KA, "pb", None),
            P(KA, "pb", None),
            P("pb", None),
        ),
        out_specs=P(KA, None),
        check_vma=False,
    )
```

profile of v0, /device:TPU:8, one launch (start us, length us, event | category | flops | bytes accessed | tf_op | source)
XLA Modules:
  0.0 292.8 jit_solution(2457836625856387109)
XLA Ops:
  0.9 38.1 %all_to_all.63 = f32[64,2,16,128]{3,2,1,0:T(8,128)S(1)} all-to-all(f32[64,2,16,128]{3,2,1,0:T(8,128)S(1)} %broadcast_in_dim.6), channel_id=1, replica_groups=mesh['ka_0'=4,'ka_1'=4,'ka_2'=4,'ka_3'=2,'pb'=4] {'ka_0','ka_1','ka_2'}, dimensions={0} | all-to-all | bytes 2097152 | tf_op jit(solution)/shard_map/all_to_all | solution.py:21
  39.2 5.4 %all_to_all.64 = f32[2,64,2,16,128]{4,3,2,1,0:T(8,128)S(1)} all-to-all(f32[2,64,2,16,128]{4,3,2,1,0:T(8,128)S(1)} %broadcast_in_dim.7), channel_id=1, replica_groups=mesh['ka_0'=4,'ka_1'=4,'ka_2'=4,'ka_3'=2,'pb'=4] {'ka_3'}, dimensions={0} | all-to-all | bytes 4194304 | tf_op jit(solution)/shard_map/all_to_all | solution.py:21
  45.8 1.9 copy.118
  47.7 2.8 fusion.69
  51.2 12.8 %all-to-all-start.2 = ((f32[2,16,16,128]{3,2,0,1:T(8,128)}), f32[2,16,16,128]{3,2,0,1:T(8,128)S(1)}, u32[]{:S(2)}, u32[]{:S(2)}) async-start(f32[2,16,16,128]{3,2,0,1:T(8,128)} %copy.119), calls=%async_computation.2 | async-start | bytes 524288 | tf_op jit(solution)/shard_map/all_to_all | solution.py:139
  64.8 15.0 %all-to-all-done.2 = f32[2,16,16,128]{3,2,0,1:T(8,128)S(1)} async-done(((f32[2,16,16,128]{3,2,0,1:T(8,128)}), f32[2,16,16,128]{3,2,0,1:T(8,128)S(1)}, u32[]{:S(2)}, u32[]{:S(2)}) %all-to-all-start.2) | async-done | bytes 262176 | tf_op jit(solution)/shard_map/all_to_all | solution.py:139
  85.6 16.3 %copy.127 = f32[2,2,4,2,4096]{2,3,1,0,4:T(2,128)} copy(f32[2,2,4,2,4096]{4,3,2,0,1:T(2,128)S(1)} %pad_maximum_fusion) | data formatting | bytes 1048576 | tf_op jit(solution)/shard_map/stack | solution.py:151
  101.9 27.6 %reshape.193 = f32[128,1,1024]{2,1,0:T(1,128)} reshape(f32[4096,2,2,2,4]{4,3,2,1,0:T(2,128)} %bitcast.132) | data formatting | bytes 1048576
  129.5 13.6 %all-to-all-start.3 = ((f32[128,1,1024]{2,1,0:T(1,128)}), f32[128,1,1024]{2,1,0:T(1,128)S(1)}, u32[]{:S(2)}, u32[]{:S(2)}) async-start(f32[128,1,1024]{2,1,0:T(1,128)} %reshape.193), calls=%async_computation.3 | async-start | bytes 1048576 | tf_op jit(solution)/shard_map/all_to_all | solution.py:154
  143.1 17.9 %all-to-all-done.3 = f32[128,1,1024]{2,1,0:T(1,128)S(1)} async-done(((f32[128,1,1024]{2,1,0:T(1,128)}), f32[128,1,1024]{2,1,0:T(1,128)S(1)}, u32[]{:S(2)}, u32[]{:S(2)}) %all-to-all-start.3) | async-done | bytes 524320 | tf_op jit(solution)/shard_map/all_to_all | solution.py:154
  161.5 1.9 reduce
  163.4 27.3 %reshape.194 = f32[4096,2,2,2,4]{4,3,2,1,0:T(2,128)} reshape(f32[128,1024]{1,0:T(8,128)S(1)} %reduce) | data formatting | bytes 1048576
  190.7 22.3 %copy.154 = f32[2,2,4,2,128,32]{5,4,3,2,1,0:T(8,128)S(1)} copy(f32[2,2,4,2,128,32]{2,3,1,0,5,4:T(2,128)} %bitcast.133) | data formatting | bytes 1048576 | tf_op jit(solution)/shard_map/all_to_all | solution.py:154
  213.0 3.0 %copy.129 = f32[128,2,2,4,2,32]{5,4,3,1,0,2:T(2,128)} copy(f32[128,2,2,4,2,32]{5,0,4,3,2,1:T(8,128)S(1)} %bitcast.134) | data formatting | bytes 1048576 | tf_op jit(solution)/shard_map/all_to_all | solution.py:154
  215.9 4.0 %reshape.181 = f32[256,2,256]{2,0,1:T(8,128)S(1)} reshape(f32[128,2,2,4,2,32]{5,4,3,1,0,2:T(2,128)} %copy.129) | data formatting | bytes 1048576 | tf_op jit(solution)/shard_map/reshape | solution.py:155
  219.9 1.5 fusion.34
  221.4 1.5 fusion.35
  222.9 1.5 convolution_subtract_fusion.4
  224.4 1.5 convolution_add_fusion.4
  225.9 1.6 fusion.56
  227.6 1.6 fusion.54
  229.2 1.6 convolution_subtract_fusion.3
  230.8 1.9 convolution_add_fusion.3
  232.7 1.5 copy.130
  234.3 2.8 reshape.195
  237.1 6.6 %all-to-all-start.4 = ((f32[128,1,1024]{2,1,0:T(1,128)}), f32[128,1,1024]{2,1,0:T(1,128)S(1)}, u32[]{:S(2)}, u32[]{:S(2)}) async-start(f32[128,1,1024]{2,1,0:T(1,128)} %reshape.195), calls=%async_computation.4 | async-start | bytes 1048576 | tf_op jit(solution)/shard_map/all_to_all | solution.py:160
  244.4 17.5 %all-to-all-done.4 = f32[128,1,1024]{2,1,0:T(1,128)S(1)} async-done(((f32[128,1,1024]{2,1,0:T(1,128)}), f32[128,1,1024]{2,1,0:T(1,128)S(1)}, u32[]{:S(2)}, u32[]{:S(2)}) %all-to-all-start.4) | async-done | bytes 524320 | tf_op jit(solution)/shard_map/all_to_all | solution.py:160
  261.8 1.9 reduce.1
  263.7 1.8 reshape.196
  266.2 1.6 copy.155
  267.8 1.8 reshape.192
  275.2 15.8 %all_to_all.65 = f32[4,1,128]{2,1,0:T(1,128)S(1)} all-to-all(f32[4,1,128]{2,1,0:T(1,128)S(1)} %reshape.197), channel_id=1, replica_groups=mesh['ka_0'=4,'ka_1'=4,'ka_2'=4,'ka_3'=2,'pb'=4] {'pb'}, dimensions={0} | all-to-all | bytes 4096 | tf_op jit(solution)/shard_map/all_to_all | solution.py:21
  (69 shorter events, 18.1 us)
Async XLA Ops:
  0.0 64.2 %copy-start = (f32[2,4,2,64,128]{4,3,2,1,0:T(8,128)S(1)}, f32[2,4,2,64,128]{4,3,2,1,0:T(8,128)}, u32[]{:S(2)}) copy-start(f32[2,4,2,64,128]{4,3,2,1,0:T(8,128)} %param.10) | copy-start | bytes 1572868
  45.8 1.9 copy-start.9
  47.7 16.4 %copy-start.4 = (f32[2,64,128]{2,1,0:T(8,128)S(1)}, f32[2,64,128]{2,1,0:T(8,128)}, u32[]{:S(2)}) copy-start(f32[2,64,128]{2,1,0:T(8,128)} %param.11) | copy-start | bytes 196612
  51.2 28.6 %all-to-all-start.2 = ((f32[2,16,16,128]{3,2,0,1:T(8,128)}), f32[2,16,16,128]{3,2,0,1:T(8,128)S(1)}, u32[]{:S(2)}, u32[]{:S(2)}) async-start(f32[2,16,16,128]{3,2,0,1:T(8,128)} %copy.119), calls=%async_computation.2 | async-start | bytes 524288 | tf_op jit(solution)/shard_map/all_to_all | solution.py:139
  101.9 41.2 %copy-start.8 = (s32[3,256]{1,0:T(4,128)S(1)}, s32[3,256]{1,0:T(4,128)}, u32[]{:S(2)}) copy-start(s32[3,256]{1,0:T(4,128)} %param.13) | copy-start | bytes 9220
  129.5 31.5 %all-to-all-start.3 = ((f32[128,1,1024]{2,1,0:T(1,128)}), f32[128,1,1024]{2,1,0:T(1,128)S(1)}, u32[]{:S(2)}, u32[]{:S(2)}) async-start(f32[128,1,1024]{2,1,0:T(1,128)} %reshape.193), calls=%async_computation.3 | async-start | bytes 1048576 | tf_op jit(solution)/shard_map/all_to_all | solution.py:154
  234.2 9.5 %copy-start.7 = (f32[4,2]{0,1:T(2,128)S(1)}, f32[4,2]{0,1:T(2,128)}, u32[]{:S(2)}) copy-start(f32[4,2]{0,1:T(2,128)} %param.19) | copy-start | bytes 100
  234.2 9.8 %copy-start.6 = (s32[2,4,64]{2,1,0:T(4,128)S(1)}, s32[2,4,64]{2,1,0:T(4,128)}, u32[]{:S(2)}) copy-start(s32[2,4,64]{2,1,0:T(4,128)} %param.18) | copy-start | bytes 6148
  234.3 9.9 %copy-start.5 = (f32[2,4,64]{2,1,0:T(4,128)S(1)}, f32[2,4,64]{2,1,0:T(4,128)}, u32[]{:S(2)}) copy-start(f32[2,4,64]{2,1,0:T(4,128)} %param.17) | copy-start | bytes 6148
  234.3 9.9 %copy-start.10 = (f32[2,64]{1,0:T(2,128)S(1)}, f32[2,64]{1,0:T(2,128)}, u32[]{:S(2)}) copy-start(f32[2,64]{1,0:T(2,128)} %param.16) | copy-start | bytes 1540
  237.1 24.7 %all-to-all-start.4 = ((f32[128,1,1024]{2,1,0:T(1,128)}), f32[128,1,1024]{2,1,0:T(1,128)S(1)}, u32[]{:S(2)}, u32[]{:S(2)}) async-start(f32[128,1,1024]{2,1,0:T(1,128)} %reshape.195), calls=%async_computation.4 | async-start | bytes 1048576 | tf_op jit(solution)/shard_map/all_to_all | solution.py:160
  267.8 1.8 copy-start.3
  270.3 1.9 copy-start.2
  274.1 18.2 %copy-start.1 = (f32[2,4,2,64,128]{4,3,2,1,0:T(8,128)S(1)}, f32[2,4,2,64,128]{4,3,2,1,0:T(8,128)}, u32[]{:S(2)}) copy-start(f32[2,4,2,64,128]{4,3,2,1,0:T(8,128)} %param.10) | copy-start | bytes 1572868
where the time goes:
time: 297 us; the launch traced here: 293 us
  local copies, waits for them, and re-layouts  118 us (40%)
  blocking collectives  59.3 us (20%)
  waiting for transfers between devices  50.3 us (17%)
  starting transfers between devices  33 us (11%)
  matrix products  25.9 us (9%)
  other arithmetic  5.62 us (2%)
    unnamed x30, local copies, waits for them, and re-layouts  60.7 us
    all_to_all x3, blocking collectives, sent_to_all(): lax.all_to_all(jnp.broadcast_to(x[None], (devices, *x.shape)), axis, 0, 0...  59.3 us
    all_to_all x3, local copies, waits for them, and re-layouts, shards(): lax.all_to_all(pair_major, KA, split_axis=4, concat_axis=0, tiled=True)  25.8 us
    all_to_all x1, waiting for transfers between devices, shards(): lax.all_to_all(pair_major, KA, split_axis=4, concat_axis=0, tiled=True)  17.9 us
    all_to_all x1, waiting for transfers between devices, shards(): lax.all_to_all(fine_cols, KA, split_axis=0, concat_axis=4, tiled=True)  17.5 us
    another operation x3, local copies, waits for them, and re-layouts, shards(): jnp.stack([wannier_real, wannier_imag], 1)  16.8 us
    dot_general x9, matrix products, product(): jnp.dot(left_matrix, right_matrix, precision=PRECISE, preferred_element_t...  15.4 us
    all_to_all x1, waiting for transfers between devices, shards(): lax.all_to_all(shares, 'pb', split_axis=1, concat_axis=2, tiled=True)  15 us
  transfers between devices with their start and end apart: 3, of which 3 were waited for; matrix products, arithmetic and copies ran while one was open for 0% of the time, Pallas kernels for 0%

commit v1 on v0

--- a/solution.py
+++ b/solution.py
@@ -151,7 +151,10 @@
     pair_major = jnp.stack([wannier_real, wannier_imag], 1).reshape(
         coarse_rows, 2, qpoint_rows, branches, orbitals * orbitals
     )
-    arrived_block = lax.all_to_all(pair_major, KA, split_axis=4, concat_axis=0, tiled=True)
+    arrived_block = jnp.concatenate(
+        lax.all_to_all(jnp.stack(jnp.split(pair_major, lax.axis_size(KA), axis=4)), KA, 0, 0),
+        axis=0,
+    )
     columns = arrived_block.reshape(arrived_block.shape[0], 2, -1)
     fine_real_part, fine_imag_part = sectioned(columns[:, 0], columns[:, 1], tables)
     fine_cols = jnp.stack([fine_real_part, fine_imag_part], 1).reshape(

time: 297 us -> 214 us (0.72)
  local copies, waits for them, and re-layouts: 118 us -> 34.8 us
    unnamed x30 -> x156, local copies, waits for them, and re-layouts: 60.7 us -> 20.1 us
    all_to_all x3 -> x1, local copies, waits for them, and re-layouts: 25.8 us -> 0.51 us  [shards(): lax.all_to_all(jnp.stack(jnp.split(pair_major, lax.axis_size(KA), axis=4)...]
    another operation x3, local copies, waits for them, and re-layouts: 16.8 us -> 0.57 us  [shards(): jnp.stack([wannier_real, wannier_imag], 1)]
    reshape x1 -> x0, local copies, waits for them, and re-layouts: 4.01 us -> none  [shards(): columns = arrived_block.reshape(arrived_block.shape[0], 2, -1)]
  transfers between devices with their start and end apart: 3 -> 3, of which waited for: 3 -> 3; matrix products, arithmetic and copies ran while one was open for 0% -> 1% of each run, Pallas kernels for 0% -> 0%
where the time goes in v1:
time: 214 us; the launch traced here: 210 us
  blocking collectives  59.3 us (28%)
  waiting for transfers between devices  50.2 us (23%)
  local copies, waits for them, and re-layouts  34.8 us (16%)
  starting transfers between devices  32.7 us (15%)
  matrix products  25.8 us (12%)
  other arithmetic  5.36 us (3%)
    all_to_all x3, blocking collectives, sent_to_all(): lax.all_to_all(jnp.broadcast_to(x[None], (devices, *x.shape)), axis, 0, 0...  59.3 us
    unnamed x156, local copies, waits for them, and re-layouts  20.1 us
    all_to_all x1, waiting for transfers between devices, shards(): lax.all_to_all(jnp.stack(jnp.split(pair_major, lax.axis_size(KA), axis=4)...  18 us
    all_to_all x1, waiting for transfers between devices, shards(): lax.all_to_all(fine_cols, KA, split_axis=0, concat_axis=4, tiled=True)  17.3 us
    dot_general x9, matrix products, product(): jnp.dot(left_matrix, right_matrix, precision=PRECISE, preferred_element_t...  15.3 us
    all_to_all x1, waiting for transfers between devices, shards(): lax.all_to_all(shares, 'pb', split_axis=1, concat_axis=2, tiled=True)  14.9 us
    all_to_all x1, starting transfers between devices, shards(): lax.all_to_all(jnp.stack(jnp.split(pair_major, lax.axis_size(KA), axis=4)...  13.3 us
    all_to_all x1, starting transfers between devices, shards(): lax.all_to_all(shares, 'pb', split_axis=1, concat_axis=2, tiled=True)  12.5 us
  transfers between devices with their start and end apart: 3, of which 3 were waited for; matrix products, arithmetic and copies ran while one was open for 1% of the time, Pallas kernels for 0%

profile of v1, /device:TPU:8, one launch (start us, length us, event | category | flops | bytes accessed | tf_op | source)
XLA Modules:
  0.0 209.8 jit_solution(14012008861153002285)
XLA Ops:
  0.9 38.1 %all_to_all.53 = f32[64,2,16,128]{3,2,1,0:T(8,128)S(1)} all-to-all(f32[64,2,16,128]{3,2,1,0:T(8,128)S(1)} %broadcast_in_dim.6), channel_id=1, replica_groups=mesh['ka_0'=4,'ka_1'=4,'ka_2'=4,'ka_3'=2,'pb'=4] {'ka_0','ka_1','ka_2'}, dimensions={0} | all-to-all | bytes 2097152 | tf_op jit(solution)/shard_map/all_to_all | solution.py:21
  39.2 5.4 %all_to_all.54 = f32[2,64,2,16,128]{4,3,2,1,0:T(8,128)S(1)} all-to-all(f32[2,64,2,16,128]{4,3,2,1,0:T(8,128)S(1)} %broadcast_in_dim.7), channel_id=1, replica_groups=mesh['ka_0'=4,'ka_1'=4,'ka_2'=4,'ka_3'=2,'pb'=4] {'ka_3'}, dimensions={0} | all-to-all | bytes 4194304 | tf_op jit(solution)/shard_map/all_to_all | solution.py:21
  45.8 1.9 copy.369
  47.7 2.8 %fusion.69 = f32[2,16,16,128]{3,1,2,0:T(8,128)S(1)} fusion(f32[16,128,256,1]{2,1,0,3:T(8,128)} %bitcast.641, s32[2,16]{1,0:T(2,128)S(1)} %bitcast.650), kind=kOutput, calls=%fused_computation.226 | convolution fusion | flops 201334784 | bytes 2359424 | tf_op jit(solution)/shard_map/dot_general | solution.py:42
  51.2 12.5 %all-to-all-start.2 = ((f32[2,16,16,128]{3,2,0,1:T(8,128)}), f32[2,16,16,128]{3,2,0,1:T(8,128)S(1)}, u32[]{:S(2)}, u32[]{:S(2)}) async-start(f32[2,16,16,128]{3,2,0,1:T(8,128)} %copy.370), calls=%async_computation.2 | async-start | bytes 524288 | tf_op jit(solution)/shard_map/all_to_all | solution.py:139
  64.5 14.9 %all-to-all-done.2 = f32[2,16,16,128]{3,2,0,1:T(8,128)S(1)} async-done(((f32[2,16,16,128]{3,2,0,1:T(8,128)}), f32[2,16,16,128]{3,2,0,1:T(8,128)S(1)}, u32[]{:S(2)}, u32[]{:S(2)}) %all-to-all-start.2) | async-done | bytes 262176 | tf_op jit(solution)/shard_map/all_to_all | solution.py:139
  79.4 1.2 fusion.16
  81.6 1.1 fusion.6
  83.2 1.2 fusion.7
  95.9 3.2 %reshape.189 = f32[128,1,1024]{2,1,0:T(1,128)} reshape(f32[128,2,2,4,2,32]{5,4,3,2,1,0:T(2,128)S(1)} %copy.378) | data formatting | bytes 1048576
  99.2 13.3 %all-to-all-start.3 = ((f32[128,1,1024]{2,1,0:T(1,128)}), f32[128,1,1024]{2,1,0:T(1,128)S(1)}, u32[]{:S(2)}, u32[]{:S(2)}) async-start(f32[128,1,1024]{2,1,0:T(1,128)} %reshape.189), calls=%async_computation.3 | async-start | bytes 1048576 | tf_op jit(solution)/shard_map/all_to_all | solution.py:155
  112.5 18.0 %all-to-all-done.3 = f32[128,1,1024]{2,1,0:T(1,128)S(1)} async-done(((f32[128,1,1024]{2,1,0:T(1,128)}), f32[128,1,1024]{2,1,0:T(1,128)S(1)}, u32[]{:S(2)}, u32[]{:S(2)}) %all-to-all-start.3) | async-done | bytes 524320 | tf_op jit(solution)/shard_map/all_to_all | solution.py:155
  131.0 1.9 reduce
  132.9 1.8 reshape.190
  134.6 2.0 reshape.187
  137.1 1.5 fusion.34
  138.5 1.5 fusion.35
  140.0 1.5 convolution_subtract_fusion.4
  141.5 1.5 convolution_add_fusion.4
  143.0 1.8 fusion.56
  144.8 1.6 fusion.54
  146.4 1.6 convolution_subtract_fusion.3
  148.1 1.6 convolution_add_fusion.3
  149.7 1.5 copy.380
  151.3 2.8 %reshape.191 = f32[128,1,1024]{2,1,0:T(1,128)} reshape(f32[256,2,4,2,32]{4,3,2,1,0:T(2,128)S(1)} %copy.380) | data formatting | bytes 1048576
  154.1 6.9 %all-to-all-start.4 = ((f32[128,1,1024]{2,1,0:T(1,128)}), f32[128,1,1024]{2,1,0:T(1,128)S(1)}, u32[]{:S(2)}, u32[]{:S(2)}) async-start(f32[128,1,1024]{2,1,0:T(1,128)} %reshape.191), calls=%async_computation.4 | async-start | bytes 1048576 | tf_op jit(solution)/shard_map/all_to_all | solution.py:163
  161.7 17.3 %all-to-all-done.4 = f32[128,1,1024]{2,1,0:T(1,128)S(1)} async-done(((f32[128,1,1024]{2,1,0:T(1,128)}), f32[128,1,1024]{2,1,0:T(1,128)S(1)}, u32[]{:S(2)}, u32[]{:S(2)}) %all-to-all-start.4) | async-done | bytes 524320 | tf_op jit(solution)/shard_map/all_to_all | solution.py:163
  179.0 1.9 reduce.1
  180.9 1.8 reshape.192
  183.4 1.6 copy.405
  185.0 1.8 reshape.188
  192.4 15.8 %all_to_all.55 = f32[4,1,128]{2,1,0:T(1,128)S(1)} all-to-all(f32[4,1,128]{2,1,0:T(1,128)S(1)} %reshape.193), channel_id=1, replica_groups=mesh['ka_0'=4,'ka_1'=4,'ka_2'=4,'ka_3'=2,'pb'=4] {'pb'}, dimensions={0} | all-to-all | bytes 4096 | tf_op jit(solution)/shard_map/all_to_all | solution.py:21
  (195 shorter events, 25.1 us)
Async XLA Ops:
  0.0 63.9 %copy-start = (f32[2,4,2,64,128]{4,3,2,1,0:T(8,128)S(1)}, f32[2,4,2,64,128]{4,3,2,1,0:T(8,128)}, u32[]{:S(2)}) copy-start(f32[2,4,2,64,128]{4,3,2,1,0:T(8,128)} %param.10) | copy-start | bytes 1572868
  45.8 1.9 copy-start.8
  47.7 16.1 %copy-start.3 = (f32[2,64,128]{2,1,0:T(8,128)S(1)}, f32[2,64,128]{2,1,0:T(8,128)}, u32[]{:S(2)}) copy-start(f32[2,64,128]{2,1,0:T(8,128)} %param.11) | copy-start | bytes 196612
  51.2 28.2 %all-to-all-start.2 = ((f32[2,16,16,128]{3,2,0,1:T(8,128)}), f32[2,16,16,128]{3,2,0,1:T(8,128)S(1)}, u32[]{:S(2)}, u32[]{:S(2)}) async-start(f32[2,16,16,128]{3,2,0,1:T(8,128)} %copy.370), calls=%async_computation.2 | async-start | bytes 524288 | tf_op jit(solution)/shard_map/all_to_all | solution.py:139
  95.9 16.5 %copy-start.7 = (s32[3,256]{1,0:T(4,128)S(1)}, s32[3,256]{1,0:T(4,128)}, u32[]{:S(2)}) copy-start(s32[3,256]{1,0:T(4,128)} %param.13) | copy-start | bytes 9220
  99.2 31.3 %all-to-all-start.3 = ((f32[128,1,1024]{2,1,0:T(1,128)}), f32[128,1,1024]{2,1,0:T(1,128)S(1)}, u32[]{:S(2)}, u32[]{:S(2)}) async-start(f32[128,1,1024]{2,1,0:T(1,128)} %reshape.189), calls=%async_computation.3 | async-start | bytes 1048576 | tf_op jit(solution)/shard_map/all_to_all | solution.py:155
  151.2 9.8 %copy-start.6 = (f32[4,2]{0,1:T(2,128)S(1)}, f32[4,2]{0,1:T(2,128)}, u32[]{:S(2)}) copy-start(f32[4,2]{0,1:T(2,128)} %param.19) | copy-start | bytes 100
  151.3 10.1 %copy-start.5 = (s32[2,4,64]{2,1,0:T(4,128)S(1)}, s32[2,4,64]{2,1,0:T(4,128)}, u32[]{:S(2)}) copy-start(s32[2,4,64]{2,1,0:T(4,128)} %param.18) | copy-start | bytes 6148
  151.3 10.3 %copy-start.4 = (f32[2,4,64]{2,1,0:T(4,128)S(1)}, f32[2,4,64]{2,1,0:T(4,128)}, u32[]{:S(2)}) copy-start(f32[2,4,64]{2,1,0:T(4,128)} %param.17) | copy-start | bytes 6148
  151.3 10.3 %copy-start.9 = (f32[2,64]{1,0:T(2,128)S(1)}, f32[2,64]{1,0:T(2,128)}, u32[]{:S(2)}) copy-start(f32[2,64]{1,0:T(2,128)} %param.16) | copy-start | bytes 1540
  154.1 24.9 %all-to-all-start.4 = ((f32[128,1,1024]{2,1,0:T(1,128)}), f32[128,1,1024]{2,1,0:T(1,128)S(1)}, u32[]{:S(2)}, u32[]{:S(2)}) async-start(f32[128,1,1024]{2,1,0:T(1,128)} %reshape.191), calls=%async_computation.4 | async-start | bytes 1048576 | tf_op jit(solution)/shard_map/all_to_all | solution.py:163
  185.0 1.8 copy-start.2
  187.5 1.8 copy-start.1
